TPU v7x, 128 devices: a whole 4x4x4 slice. The times are simulated.
128 devices in a mesh: row: 4 (over y), col: 32 (over z, x, core).
Axes of the slice: x: 4, y: 4, z: 4, core: 2. Of those that a mesh axis runs over, the one named last changes fastest.
Arguments:
- tokens: bfloat16 [768, 8192], P('col', 'row'), may hold values from -6 to 6
- gate_weight: bfloat16 [8192, 28672], P('row', 'col'), may hold values from -0.0625 to 0.0625
- up_weight: bfloat16 [8192, 28672], P('row', 'col'), may hold values from -0.0625 to 0.0625
- down_weight: bfloat16 [28672, 8192], P('col', 'row'), may hold values from -0.03125 to 0.03125
- mask_gate: int32 [128, 448], P('row', 'col'), may hold values from 0 to 1, as said below
- mask_up: int32 [128, 448], P('row', 'col'), may hold values from 0 to 1, as said below
- mask_down: int32 [448, 128], P('col', 'row'), may hold values from 0 to 1, as said below
- cotangent: bfloat16 [768, 8192], P('col', 'row'), may hold values from -1.5 to 1.5
Outputs:
- output: bfloat16 [768, 8192], P('col', 'row')
- grad_input: bfloat16 [768, 8192], P('col', 'row')
- grad_gate: bfloat16 [8192, 28672], P('row', 'col')
- grad_up: bfloat16 [8192, 28672], P('row', 'col')
- grad_down: bfloat16 [28672, 8192], P('col', 'row')
Inputs may be any that keep to these rules, and one draw needn't show every extreme that they name: `mask_gate`: 1 where a 64 x 64 block of the weight is kept, 0 where it is pruned. `mask_up`: 1 where a 64 x 64 block of the weight is kept, 0 where it is pruned. `mask_down`: 1 where a 64 x 64 block of the weight is kept, 0 where it is pruned.
All inputs are finite; a program needn't handle non-finite values.
Results may differ from a plain program's by a relative error of at most 0.006.
Values may be sent and summed in bfloat16 or wider, within the bound.
No kernel may reach another device: no remote copies, remote signals or barrier semaphores. Data moves between devices by JAX's collectives and lax.ppermute only.
A program may use at most 128 MiB of HBM per device.

v0:
```python
import jax
import jax.numpy as jnp
from jax import lax
from jax.sharding import PartitionSpec as P

BLOCK = 64


def expand(mask):
    return jnp.repeat(jnp.repeat(mask, BLOCK, 0), BLOCK, 1).astype(jnp.bfloat16)


def contract_last(left, right):
    return lax.dot_general(
        left, right, (((1,), (1,)), ((), ())), preferred_element_type=jnp.float32
    )


def contract_first(left, right):
    return lax.dot_general(
        left, right, (((0,), (0,)), ((), ())), preferred_element_type=jnp.float32
    )


def backward_gates(dhid, gate, up):
    sigma = jax.nn.sigmoid(gate)
    dgate = (dhid * up * sigma * (1.0 + gate * (1.0 - sigma))).astype(jnp.bfloat16)
    dup = (dhid * gate * sigma).astype(jnp.bfloat16)
    return (dgate, dup)


def body(tokens, gate_weight, up_weight, down_weight, mask_gate, mask_up, mask_down, cotangent):
    keep_gate = expand(mask_gate)
    keep_up = expand(mask_up)
    keep_down = expand(mask_down)
    w_gate = gate_weight * keep_gate
    w_up = up_weight * keep_up
    w_down = down_weight * keep_down
    width = w_gate.shape[1]
    panel = lax.all_gather(tokens, "col", axis=0, tiled=True)
    stacked = jnp.concatenate([w_gate, w_up], axis=1)
    partial_both = jnp.dot(panel, stacked, preferred_element_type=jnp.float32)
    summed = lax.psum(partial_both, "row")
    gate = summed[:, :width]
    up = summed[:, width:]
    hidden = (jax.nn.silu(gate) * up).astype(jnp.bfloat16)
    output = lax.psum_scatter(
        jnp.dot(hidden, w_down, preferred_element_type=jnp.float32),
        "col",
        scatter_dimension=0,
        tiled=True,
    ).astype(jnp.bfloat16)
    cot_panel = lax.all_gather(cotangent, "col", axis=0, tiled=True)
    partial_dhid = contract_last(cot_panel, w_down)
    dhid = lax.psum(partial_dhid, "row")
    dgate, dup = backward_gates(dhid, gate, up)
    grad_down = (contract_first(hidden, cot_panel) * keep_down).astype(jnp.bfloat16)
    grad_gate = (contract_first(panel, dgate) * keep_gate).astype(jnp.bfloat16)
    grad_up = (contract_first(panel, dup) * keep_up).astype(jnp.bfloat16)
    grad_input = lax.psum_scatter(
        contract_last(dgate, w_gate) + contract_last(dup, w_up),
        "col",
        scatter_dimension=0,
        tiled=True,
    ).astype(jnp.bfloat16)
    return (output, grad_input, grad_gate, grad_up, grad_down)


def solution(mesh):
    return jax.shard_map(
        body,
        mesh=mesh,
        in_specs=(
            P("col", "row"),
            P("row", "col"),
            P("row", "col"),
            P("col", "row"),
            P("row", "col"),
            P("row", "col"),
            P("col", "row"),
            P("col", "row"),
        ),
        out_specs=(
            P("col", "row"),
            P("col", "row"),
            P("row", "col"),
            P("row", "col"),
            P("col", "row"),
        ),
        check_vma=False,
    )
```

profile of v0, /device:TPU:0, one launch (start us, length us, event | category | flops | bytes accessed | tf_op | source)
XLA Modules:
  0.0 471.1 jit_solution(7040883705480512886)
XLA Ops:
  7.2 0.0 all-gather.5.cloned.1.call-start
  7.2 0.7 all-gather.5.cloned.1.call-update
  7.9 0.0 all-gather.3.cloned.1.call-start
  7.9 0.7 all-gather.3.cloned.1.call-update
  8.6 0.0 all-reduce.3.cloned.1.call-start
  8.7 0.7 convert_element_type.66
  9.4 0.1 broadcast_in_dim.18
  9.5 0.1 convert_element_type.67
  9.7 0.7 convert_element_type.69
  10.4 0.1 broadcast_in_dim.20
  10.5 0.1 convert_element_type.70
  10.7 6.1 %copy.24 = bf16[2048,896]{0,1:T(8,128)(2,1)} copy(bf16[2048,896]{1,0:T(8,128)(2,1)} %param.9) | data formatting | bytes 7340032 | tf_op args[1]
  16.7 0.0 copy-start.5
  16.7 6.1 %copy.25 = bf16[2048,896]{0,1:T(8,128)(2,1)} copy(bf16[2048,896]{1,0:T(8,128)(2,1)} %param.10) | data formatting | bytes 7340032 | tf_op args[2]
  22.8 0.0 copy-done.5
  22.8 0.1 copy.26
  22.9 0.1 broadcast_in_dim.22
  23.0 0.1 convert_element_type.74
  23.2 6.1 %copy.27 = bf16[896,2048]{0,1:T(8,128)(2,1)} copy(bf16[896,2048]{1,0:T(8,128)(2,1)} %param.11) | data formatting | bytes 7340032 | tf_op args[3]
  29.2 0.0 copy-start
  29.2 0.0 copy-start.1
  29.2 4.4 bitcast_multiply_fusion.4
  33.7 0.0 copy-done
  33.7 1.2 copy-done.1
  34.8 3.6 bitcast_multiply_fusion.2
  38.4 19.3 %all-gather.5.cloned.1.call-done = bf16[768,2048]{1,0:T(8,128)(2,1)} async-done(((bf16[24,2048]{1,0:T(8,128)(2,1)}), bf16[768,2048]{1,0:T(8,128)(2,1)}) %all-gather.5.cloned.1.call-update) | async-done | bytes 3145744 | tf_op jit(solution)/shard_map/all_gather | solution.py:53
  57.7 7.6 %convolution_bitcast_fusion = f32[768,896]{0,1:T(8,128)} fusion(bf16[896,2048]{0,1:T(8,128)(2,1)} %bitcast_multiply_fusion.4, bf16[768,2048]{1,0:T(8,128)(2,1)} %all-gather.5.cloned.1.call-done), kind=kOutput, calls=%fused_computation.18 | convolution fusion | flops 2818572288 | bytes 9568256 | tf_op jit(solution)/shard_map/dot_general | solution.py:14
  65.3 38.9 %all-gather.3.cloned.1.call-done = bf16[768,2048]{1,0:T(8,128)(2,1)} async-done(((bf16[24,2048]{1,0:T(8,128)(2,1)}), bf16[768,2048]{1,0:T(8,128)(2,1)}) %all-gather.3.cloned.1.call-update) | async-done | bytes 3145744 | tf_op jit(solution)/shard_map/all_gather | solution.py:40
  104.2 12.3 %fusion.6 = f32[768,1792]{0,1:T(8,128)} fusion(bf16[768,2048]{1,0:T(8,128)(2,1)} %all-gather.3.cloned.1.call-done, bf16[2048,896]{0,1:T(8,128)(2,1)} %get-tuple-element.25, bf16[2048,896]{0,1:T(8,128)(2,1)} %get-tuple-element.26), kind=kOutput, calls=%fused_computation.11 | convolution fusion | flops 5651824640 | bytes 15990784 | tf_op jit(solution)/shard_map/dot_general | solution.py:42
  116.5 0.0 all-reduce.3.cloned.1.call-update
  116.5 0.2 reduce-scatter.5.cloned.1.call-start
  116.8 157.3 %all-reduce.3.cloned.1.call-done = (f32[768,1792]{0,1:T(8,128)}, f32[768,896]{0,1:T(8,128)}) async-done(((f32[768,1792]{0,1:T(8,128)}, f32[768,896]{0,1:T(8,128)}), (f32[768,1792]{0,1:T(8,128)}, f32[768,896]{0,1:T(8,128)})) %all-reduce.3.cloned.1.call-update) | async-done | bytes 8257552 | tf_op jit(solution)/shard_map/psum | solution.py:43
  274.0 0.0 copy-start.3
  274.0 4.3 multiply_convert_fusion.1
  278.3 0.0 copy-start.4
  278.3 0.1 copy-done.3
  278.5 0.0 copy-start.2
  278.5 3.5 fusion.11
  282.0 0.0 copy-done.4
  282.0 0.0 copy-done.2
  282.0 5.4 %convolution_add_fusion = f32[768,2048]{1,0:T(8,128)} fusion(f32[768,2048]{1,0:T(8,128)S(1)} %fusion.11, bf16[768,896]{0,1:T(8,128)(2,1)S(1)} %get-tuple-element.22, bf16[2048,896]{0,1:T(8,128)(2,1)S(1)} %copy-done.2), kind=kOutput, calls=%fused_computation.12 | convolution fusion | flops 2820145152 | bytes 17629184 | tf_op jit(solution)/shard_map/dot_general | solution.py:14
  287.4 0.0 reduce-scatter.5.cloned.1.call-update
  287.5 0.0 reduce-scatter.3.cloned.1.call-start
  287.5 7.4 %fusion.10 = f32[768,2048]{1,0:T(8,128)} fusion(bf16[768,896]{0,1:T(8,128)(2,1)S(1)} %get-tuple-element.24, bf16[896,2048]{0,1:T(8,128)(2,1)} %bitcast_multiply_fusion.4), kind=kOutput, calls=%fused_computation.20 | convolution fusion | flops 2818572288 | bytes 11337728 | tf_op jit(solution)/shard_map/dot_general | solution.py:48
  294.9 0.0 reduce-scatter.3.cloned.1.call-update
  295.0 2.1 broadcast_in_dim.23
  297.1 6.2 %copy.28 = bf16[896,2048]{1,0:T(8,128)(2,1)} copy(bf16[896,2048]{0,1:T(8,128)(2,1)} %bitcast.41) | data formatting | bytes 7340032 | tf_op jit(solution)/shard_map/convert_element_type | solution.py:10
  303.3 7.3 %fusion.5 = bf16[2048,896]{0,1:T(8,128)(2,1)} fusion(bf16[768,896]{0,1:T(8,128)(2,1)} %copy-done.4, bf16[768,2048]{1,0:T(8,128)(2,1)} %all-gather.3.cloned.1.call-done, bf16[2048,14]{0,1:T(8,128)(2,1)S(1)} %convert_element_type.67), kind=kOutput, calls=%fused_computation.7 | convolution fusion | flops 2824077312 | bytes 8249344 | tf_op jit(solution)/shard_map/dot_general | solution.py:20
  310.6 6.2 %copy.29 = bf16[2048,896]{1,0:T(8,128)(2,1)} copy(bf16[2048,896]{0,1:T(8,128)(2,1)} %fusion.5) | data formatting | bytes 7340032
  316.8 6.9 %fusion.4 = bf16[2048,896]{0,1:T(8,128)(2,1)} fusion(bf16[768,896]{0,1:T(8,128)(2,1)S(1)} %get-tuple-element.22, bf16[768,2048]{1,0:T(8,128)(2,1)} %all-gather.3.cloned.1.call-done, bf16[2048,14]{0,1:T(8,128)(2,1)S(1)} %convert_element_type.70), kind=kOutput, calls=%fused_computation.5 | convolution fusion | flops 2824077312 | bytes 8249344 | tf_op jit(solution)/shard_map/dot_general | solution.py:20
  323.7 6.1 %copy.30 = bf16[2048,896]{1,0:T(8,128)(2,1)} copy(bf16[2048,896]{0,1:T(8,128)(2,1)} %fusion.4) | data formatting | bytes 7340032
  329.8 6.9 %multiply_convert_fusion = bf16[896,2048]{1,0:T(8,128)(2,1)} fusion(bf16[896,2048]{1,0:T(8,128)(2,1)} %copy.28, bf16[768,896]{0,1:T(8,128)(2,1)S(1)} %get-tuple-element.24, bf16[768,2048]{1,0:T(8,128)(2,1)} %all-gather.5.cloned.1.call-done), kind=kOutput, calls=%fused_computation.8 | convolution fusion | flops 2824077312 | bytes 11862016 | tf_op jit(solution)/shard_map/dot_general | solution.py:20
  336.6 37.1 %reduce-scatter.5.cloned.1.call-done = f32[24,2048]{1,0:T(8,128)} async-done(((f32[768,2048]{1,0:T(8,128)}), f32[24,2048]{1,0:T(8,128)}) %reduce-scatter.5.cloned.1.call-update) | async-done | bytes 196624 | tf_op jit(solution)/shard_map/reduce_scatter | solution.py:60
  373.8 1.6 convert_element_type.79
  375.3 87.7 %reduce-scatter.3.cloned.1.call-done = f32[24,2048]{1,0:T(8,128)} async-done(((f32[768,2048]{1,0:T(8,128)}), f32[24,2048]{1,0:T(8,128)}) %reduce-scatter.3.cloned.1.call-update) | async-done | bytes 196624 | tf_op jit(solution)/shard_map/reduce_scatter | solution.py:47
  463.0 1.6 convert_element_type.76
  (1 shorter events, 0.0 us)
Async XLA Ops:
  7.2 50.5 %all-gather.5.cloned.1.call-start = ((), (), s32[]{:S(2)}) async-start(), calls=%async_computation.4 | async-start | bytes 3244032 | tf_op jit(solution)/shard_map/all_gather | solution.py:53
  7.9 96.3 %all-gather.3.cloned.1.call-start = ((), (), s32[]{:S(2)}) async-start(), calls=%async_computation.2 | async-start | bytes 3244032 | tf_op jit(solution)/shard_map/all_gather | solution.py:40
  8.6 265.4 %all-reduce.3.cloned.1.call-start = ((), (), s32[]{:S(2)}) async-start(), calls=%async_computation.6 | async-start | bytes 16515072 | tf_op jit(solution)/shard_map/psum | solution.py:43
  16.7 6.1 %copy-start.5 = (s32[14,32]{1,0:T(8,128)S(1)}, s32[14,32]{1,0:T(8,128)}, u32[]{:S(2)}) copy-start(s32[14,32]{1,0:T(8,128)} %param.14) | copy-start | bytes 5380
  29.2 4.4 copy-start
  29.2 5.6 %copy-start.1 = (bf16[2048,896]{0,1:T(8,128)(2,1)S(1)}, bf16[2048,896]{0,1:T(8,128)(2,1)}, u32[]{:S(2)}) copy-start(bf16[2048,896]{0,1:T(8,128)(2,1)} %copy.25) | copy-start | bytes 11010052
  116.5 257.2 %reduce-scatter.5.cloned.1.call-start = ((), (), s32[]{:S(2)}) async-start(), calls=%async_computation.5 | async-start | bytes 6488064 | tf_op jit(solution)/shard_map/reduce_scatter | solution.py:60
  274.0 4.5 copy-start.3
  278.3 3.7 copy-start.4
  278.5 3.5 copy-start.2
  287.5 175.6 %reduce-scatter.3.cloned.1.call-start = ((), (), s32[]{:S(2)}) async-start(), calls=%async_computation.3 | async-start | bytes 6488064 | tf_op jit(solution)/shard_map/reduce_scatter | solution.py:47
Sparse Core Ops, SparseCore 0:
  10.2 47.4 all-gather.4
  59.9 44.1 all-gather.2
  116.7 157.3 all-reduce.2
  287.6 86.1 reduce-scatter.4
  377.4 85.6 reduce-scatter.2
where the time goes:
time: 472 us; the launch traced here: 471 us
  waiting for transfers between devices  342 us (72%)
  matrix products  57.4 us (12%)
  local copies, waits for them, and re-layouts  41 us (9%)
  other arithmetic  16.9 us (4%)
  between operations  13.9 us (3%)
    psum x1, waiting for transfers between devices, body(): summed = lax.psum(partial_both, 'row')  157 us
    reduce_scatter x1, waiting for transfers between devices, body(): lax.psum_scatter(jnp.dot(hidden, w_down, preferred_element_type=jnp.float...  87.7 us
    all_gather x1, waiting for transfers between devices, body(): panel = lax.all_gather(tokens, 'col', axis=0, tiled=True)  38.9 us
    reduce_scatter x1, waiting for transfers between devices, body(): lax.psum_scatter(contract_last(dgate, w_gate) + contract_last(dup, w_up),...  37.1 us
    unnamed x17, local copies, waits for them, and re-layouts  31.7 us
    dot_general x3, matrix products, contract_first(): lax.dot_general(left, right, (((0,), (0,)), ((), ())), preferred_element_...  21.1 us
    all_gather x1, waiting for transfers between devices, body(): cot_panel = lax.all_gather(cotangent, 'col', axis=0, tiled=True)  19.3 us
    dot_general x3, matrix products, contract_last(): lax.dot_general(left, right, (((1,), (1,)), ((), ())), preferred_element_...  16.5 us
  transfers between devices with their start and end apart: 5, of which 5 were waited for; matrix products, arithmetic and copies ran while one was open for 18% of the time, Pallas kernels for 0%

commit v1 on v0

--- a/solution.py
+++ b/solution.py
@@ -37,32 +37,49 @@
     w_up = up_weight * keep_up
     w_down = down_weight * keep_down
     width = w_gate.shape[1]
-    panel = lax.all_gather(tokens, "col", axis=0, tiled=True)
-    stacked = jnp.concatenate([w_gate, w_up], axis=1)
-    partial_both = jnp.dot(panel, stacked, preferred_element_type=jnp.float32)
-    summed = lax.psum(partial_both, "row")
-    gate = summed[:, :width]
-    up = summed[:, width:]
+    pair = lax.all_gather(
+        jnp.concatenate([tokens, cotangent], axis=1), "col", axis=0, tiled=True
+    )
+    depth = tokens.shape[1]
+    panel = pair[:, :depth]
+    cot_panel = pair[:, depth:]
+    parts = jnp.concatenate(
+        [
+            jnp.dot(panel, w_gate, preferred_element_type=jnp.float32).astype(jnp.bfloat16),
+            jnp.dot(panel, w_up, preferred_element_type=jnp.float32).astype(jnp.bfloat16),
+            contract_last(cot_panel, w_down).astype(jnp.bfloat16),
+        ],
+        axis=1,
+    )
+    rows = parts.shape[0] // 4
+    swapped = lax.all_to_all(parts, "row", 0, 0, tiled=True)
+    total = jnp.sum(swapped.reshape(4, rows, 3 * width).astype(jnp.float32), axis=0)
+    gate = total[:, :width]
+    up = total[:, width : 2 * width]
+    dhid = total[:, 2 * width :]
     hidden = (jax.nn.silu(gate) * up).astype(jnp.bfloat16)
-    output = lax.psum_scatter(
-        jnp.dot(hidden, w_down, preferred_element_type=jnp.float32),
-        "col",
-        scatter_dimension=0,
-        tiled=True,
-    ).astype(jnp.bfloat16)
-    cot_panel = lax.all_gather(cotangent, "col", axis=0, tiled=True)
-    partial_dhid = contract_last(cot_panel, w_down)
-    dhid = lax.psum(partial_dhid, "row")
     dgate, dup = backward_gates(dhid, gate, up)
+    whole = lax.all_gather(
+        jnp.concatenate([hidden, dgate, dup], axis=1), "row", axis=0, tiled=True
+    )
+    hidden = whole[:, :width]
+    dgate = whole[:, width : 2 * width]
+    dup = whole[:, 2 * width :]
+    both = jnp.concatenate(
+        [
+            jnp.dot(hidden, w_down, preferred_element_type=jnp.float32).astype(jnp.bfloat16),
+            (contract_last(dgate, w_gate) + contract_last(dup, w_up)).astype(jnp.bfloat16),
+        ],
+        axis=1,
+    )
+    spread = lax.all_to_all(both, "col", 0, 0, tiled=True)
     grad_down = (contract_first(hidden, cot_panel) * keep_down).astype(jnp.bfloat16)
     grad_gate = (contract_first(panel, dgate) * keep_gate).astype(jnp.bfloat16)
     grad_up = (contract_first(panel, dup) * keep_up).astype(jnp.bfloat16)
-    grad_input = lax.psum_scatter(
-        contract_last(dgate, w_gate) + contract_last(dup, w_up),
-        "col",
-        scatter_dimension=0,
-        tiled=True,
-    ).astype(jnp.bfloat16)
+    spread = spread.reshape(-1, tokens.shape[0], 2 * depth).astype(jnp.float32)
+    owned = jnp.sum(spread, axis=0).astype(jnp.bfloat16)
+    output = owned[:, :depth]
+    grad_input = owned[:, depth:]
     return (output, grad_input, grad_gate, grad_up, grad_down)
 
 

time: 472 us -> 290 us (0.61)
  waiting for transfers between devices: 342 us -> 102 us
  blocking collectives: 0 us -> 52.6 us
  matrix products: 57.4 us -> 45.3 us
  starting transfers between devices: 0.38 us -> 7.65 us
  local copies, waits for them, and re-layouts: 41 us -> 46.2 us
    psum x1 -> x0, waiting for transfers between devices: 157 us -> none  [body(): summed = lax.psum(partial_both, 'row')]
    reduce_scatter x2 -> x0, waiting for transfers between devices: 125 us -> none  [the longest x1 87.7 us: body(): lax.psum_scatter(jnp.dot(hidden, w_down, preferred_element_type=jnp.float...]
    all_to_all x0 -> x1, blocking collectives: none -> 52.6 us  [body(): swapped = lax.all_to_all(parts, 'row', 0, 0, tiled=True)]
    all_to_all x0 -> x1, waiting for transfers between devices: none -> 33.9 us  [body(): spread = lax.all_to_all(both, 'col', 0, 0, tiled=True)]
    unnamed x17 -> x33, local copies, waits for them, and re-layouts: 31.7 us -> 19.5 us
    convert_element_type x5 -> x7, local copies, waits for them, and re-layouts: 6.74 us -> 18.9 us  [expand(): return jnp.repeat(jnp.repeat(mask, BLOCK, 0), BLOCK, 1).astype(jnp.bfloat16)]
    all_gather x2, waiting for transfers between devices: 58.1 us -> 67.9 us  [the longest x1 44.7 us: body(): lax.all_gather(jnp.concatenate([hidden, dgate, dup], axis=1), 'row', axis...]
    all_to_all x0 -> x1, starting transfers between devices: none -> 7.57 us  [body(): spread = lax.all_to_all(both, 'col', 0, 0, tiled=True)]
  transfers between devices with their start and end apart: 5 -> 3, of which waited for: 5 -> 3; matrix products, arithmetic and copies ran while one was open for 18% -> 25% of each run, Pallas kernels for 0% -> 0%
where the time goes in v1:
time: 290 us; the launch traced here: 289 us
  waiting for transfers between devices  102 us (35%)
  blocking collectives  52.6 us (18%)
  local copies, waits for them, and re-layouts  46.2 us (16%)
  matrix products  45.3 us (16%)
  other arithmetic  20.9 us (7%)
  between operations  14.3 us (5%)
  starting transfers between devices  7.65 us (3%)
    all_to_all x1, blocking collectives, body(): swapped = lax.all_to_all(parts, 'row', 0, 0, tiled=True)  52.6 us
    all_gather x1, waiting for transfers between devices, body(): lax.all_gather(jnp.concatenate([hidden, dgate, dup], axis=1), 'row', axis...  44.7 us
    all_to_all x1, waiting for transfers between devices, body(): spread = lax.all_to_all(both, 'col', 0, 0, tiled=True)  33.9 us
    all_gather x1, waiting for transfers between devices, body(): lax.all_gather(jnp.concatenate([tokens, cotangent], axis=1), 'col', axis=...  23.2 us
    unnamed x33, local copies, waits for them, and re-layouts  19.5 us
    convert_element_type x7, local copies, waits for them, and re-layouts, expand(): return jnp.repeat(jnp.repeat(mask, BLOCK, 0), BLOCK, 1).astype(jnp.bfloat16)  18.9 us
    dot_general x3, matrix products, contract_first(): lax.dot_general(left, right, (((0,), (0,)), ((), ())), preferred_element_...  18.7 us
    dot_general x3, matrix products, contract_last(): lax.dot_general(left, right, (((1,), (1,)), ((), ())), preferred_element_...  13.7 us
  transfers between devices with their start and end apart: 3, of which 3 were waited for; matrix products, arithmetic and copies ran while one was open for 25% of the time, Pallas kernels for 0%

profile of v1, /device:TPU:0, one launch (start us, length us, event | category | flops | bytes accessed | tf_op | source)
XLA Modules:
  0.0 288.6 jit_solution(12454030804781257054)
XLA Ops:
  7.2 0.0 all-gather.3.cloned.1.call-start
  7.2 1.6 pad_maximum_fusion.3
  8.8 0.0 all-gather.3.cloned.1.call-update
  8.9 0.0 all-gather.5.cloned.1.call-start
  8.9 0.7 convert_element_type.88
  9.6 0.1 copy.24
  9.7 0.1 broadcast_in_dim.22
  9.9 0.1 convert_element_type.89
  10.0 0.0 copy-start.8
  10.0 6.1 %copy.25 = bf16[896,2048]{0,1:T(8,128)(2,1)} copy(bf16[896,2048]{1,0:T(8,128)(2,1)} %param.11) | data formatting | bytes 7340032 | tf_op args[3]
  16.1 0.0 copy-done.8
  16.1 0.1 broadcast_in_dim.20
  16.2 0.2 convert_element_type.85
  16.4 0.0 copy-start.9
  16.4 6.1 %copy.23 = bf16[2048,896]{0,1:T(8,128)(2,1)} copy(bf16[2048,896]{1,0:T(8,128)(2,1)} %param.10) | data formatting | bytes 7340032 | tf_op args[2]
  22.4 0.0 copy-done.9
  22.4 0.1 broadcast_in_dim.18
  22.6 0.1 convert_element_type.81
  22.7 6.1 %copy.22 = bf16[2048,896]{0,1:T(8,128)(2,1)} copy(bf16[2048,896]{1,0:T(8,128)(2,1)} %param.9) | data formatting | bytes 7340032 | tf_op args[1]
  28.8 4.4 %bitcast_multiply_fusion = bf16[896,2048]{0,1:T(8,128)(2,1)} fusion(bf16[896,2048]{0,1:T(8,128)(2,1)} %copy.25, bf16[896,32]{0,1:T(8,128)(2,1)S(1)} %convert_element_type.89), kind=kLoop, calls=%fused_computation.17 | loop fusion | flops 1835008 | bytes 7397376 | tf_op jit(solution)/shard_map/mul | solution.py:38
  33.2 0.0 copy-done
  33.2 2.1 bitcast_multiply_fusion.1
  35.3 1.2 copy-done.1
  36.6 2.1 bitcast_multiply_fusion.2
  38.7 23.2 %all-gather.3.cloned.1.call-done = bf16[768,4096]{1,0:T(8,128)(2,1)} async-done(((bf16[24,4096]{1,0:T(8,128)(2,1)}), bf16[768,4096]{1,0:T(8,128)(2,1)}) %all-gather.3.cloned.1.call-update) | async-done | bytes 6291472 | tf_op jit(solution)/shard_map/all_gather | solution.py:40
  61.9 6.5 %fusion.15 = bf16[768,896]{1,0:T(8,128)(2,1)S(1)} fusion(bf16[896,2048]{0,1:T(8,128)(2,1)} %bitcast_multiply_fusion, bf16[768,4096]{1,0:T(8,128)(2,1)} %all-gather.3.cloned.1.call-done), kind=kOutput, calls=%fused_computation.22 | convolution fusion | flops 2819260416 | bytes 8192000 | tf_op jit(solution)/shard_map/dot_general | solution.py:14
  68.4 0.0 copy-done.2
  68.4 0.0 copy-done.10
  68.4 0.0 copy-start.4
  68.4 3.5 %fusion.12 = bf16[768,896]{1,0:T(8,128)(2,1)S(1)} fusion(bf16[2048,896]{0,1:T(8,128)(2,1)S(1)} %copy-done.2, bf16[768,4096]{1,0:T(8,128)(2,1)S(1)} %copy-done.10), kind=kOutput, calls=%fused_computation.21 | convolution fusion | flops 2819260416 | bytes 8192000 | tf_op jit(solution)/shard_map/dot_general | solution.py:49
  71.9 0.0 copy-done.4
  71.9 3.4 %fusion.9 = bf16[768,896]{1,0:T(8,128)(2,1)S(1)} fusion(bf16[2048,896]{0,1:T(8,128)(2,1)S(1)} %copy-done.4, bf16[768,4096]{1,0:T(8,128)(2,1)S(1)} %copy-done.10), kind=kOutput, calls=%fused_computation.20 | convolution fusion | flops 2819260416 | bytes 8192000 | tf_op jit(solution)/shard_map/dot_general | solution.py:48
  75.4 0.4 pad_maximum_fusion.1
  75.7 52.6 %all_to_all.18 = bf16[4,192,2688]{2,1,0:T(8,128)(2,1)S(1)} all-to-all(bf16[4,192,2688]{2,1,0:T(8,128)(2,1)S(1)} %bitcast.21), channel_id=1, replica_groups=mesh['row'=4,'col'=32] {'row'}, dimensions={0} | all-to-all | bytes 8257536 | tf_op jit(solution)/shard_map/all_to_all | solution.py:55
  128.3 0.6 convert_reduce_fusion
  128.9 0.4 multiply_convert_fusion.5
  129.3 1.0 pad_maximum_fusion.2
  130.4 0.0 all-gather.5.cloned.1.call-update
  130.4 44.7 %all-gather.5.cloned.1.call-done = bf16[768,2688]{1,0:T(8,128)(2,1)} async-done(((bf16[192,2688]{1,0:T(8,128)(2,1)}), bf16[768,2688]{1,0:T(8,128)(2,1)}) %all-gather.5.cloned.1.call-update) | async-done | bytes 4128784 | tf_op jit(solution)/shard_map/all_gather | solution.py:62
  175.1 6.0 %convolution_convert_fusion = bf16[768,2048]{1,0:T(8,128)(2,1)S(1)} fusion(bf16[896,2048]{0,1:T(8,128)(2,1)} %bitcast_multiply_fusion, bf16[768,2688]{1,0:T(8,128)(2,1)} %all-gather.5.cloned.1.call-done), kind=kOutput, calls=%fused_computation.7 | convolution fusion | flops 2820145152 | bytes 8192000 | tf_op jit(solution)/shard_map/dot_general | solution.py:70
  181.2 0.0 copy-done.5
  181.2 0.0 copy-done.11
  181.2 0.0 copy-start.3
  181.2 3.4 %fusion.21 = f32[768,2048]{1,0:T(8,128)S(1)} fusion(bf16[2048,896]{0,1:T(8,128)(2,1)S(1)} %copy-done.5, bf16[768,2688]{1,0:T(8,128)(2,1)S(1)} %copy-done.11), kind=kOutput, calls=%fused_computation.26 | convolution fusion | flops 2818572288 | bytes 11337728 | tf_op jit(solution)/shard_map/dot_general | solution.py:14
  184.6 0.0 copy-done.3
  184.6 3.7 %add_convert_fusion = bf16[768,2048]{1,0:T(8,128)(2,1)S(1)} fusion(f32[768,2048]{1,0:T(8,128)S(1)} %fusion.21, bf16[2048,896]{0,1:T(8,128)(2,1)S(1)} %copy-done.3, bf16[768,2688]{1,0:T(8,128)(2,1)S(1)} %copy-done.11), kind=kOutput, calls=%fused_computation.5 | convolution fusion | flops 2821718016 | bytes 14483456 | tf_op jit(solution)/shard_map/dot_general | solution.py:14
  188.4 3.4 %pad_maximum_fusion = bf16[768,4096]{1,0:T(8,128)(2,1)} fusion(bf16[768,2048]{1,0:T(8,128)(2,1)S(1)} %add_convert_fusion, bf16[768,2048]{1,0:T(8,128)(2,1)S(1)} %convolution_convert_fusion), kind=kLoop, calls=%fused_computation.4 | loop fusion | flops 12582912 | bytes 12582912 | tf_op jit(solution)/shard_map/concatenate | solution.py:68
  191.8 7.6 %all-to-all-start.1 = ((bf16[32,24,4096]{2,1,0:T(8,128)(2,1)}), bf16[32,24,4096]{2,1,0:T(8,128)(2,1)}, u32[]{:S(2)}, u32[]{:S(2)}) async-start(bf16[32,24,4096]{2,1,0:T(8,128)(2,1)} %bitcast.20), calls=%async_computation.1 | async-start | bytes 12582912 | tf_op jit(solution)/shard_map/all_to_all | solution.py:75
  199.3 2.1 broadcast_in_dim.23
  201.5 6.1 %copy.28 = bf16[896,2048]{1,0:T(8,128)(2,1)} copy(bf16[896,2048]{0,1:T(8,128)(2,1)} %bitcast.22) | data formatting | bytes 7340032 | tf_op jit(solution)/shard_map/convert_element_type | solution.py:10
  207.6 2.3 broadcast_in_dim.21
  209.9 6.0 %copy.27 = bf16[2048,896]{1,0:T(8,128)(2,1)} copy(bf16[2048,896]{0,1:T(8,128)(2,1)} %bitcast.23) | data formatting | bytes 7340032 | tf_op jit(solution)/shard_map/convert_element_type | solution.py:10
  215.9 2.3 broadcast_in_dim.19
  218.2 6.2 %copy.26 = bf16[2048,896]{1,0:T(8,128)(2,1)} copy(bf16[2048,896]{0,1:T(8,128)(2,1)} %bitcast.24) | data formatting | bytes 7340032 | tf_op jit(solution)/shard_map/convert_element_type | solution.py:10
  224.4 8.5 %multiply_convert_fusion = bf16[896,2048]{1,0:T(8,128)(2,1)} fusion(bf16[896,2048]{1,0:T(8,128)(2,1)} %copy.28, bf16[768,4096]{1,0:T(8,128)(2,1)} %all-gather.3.cloned.1.call-done, bf16[768,2688]{1,0:T(8,128)(2,1)} %all-gather.5.cloned.1.call-done), kind=kOutput, calls=%fused_computation.1 | convolution fusion | flops 2824077312 | bytes 11862016 | tf_op jit(solution)/shard_map/dot_general | solution.py:20
  232.9 0.0 slice-done
  232.9 0.0 copy-done.12
  232.9 0.0 copy-start.7
  232.9 5.1 %multiply_convert_fusion.1 = bf16[2048,896]{1,0:T(8,128)(2,1)} fusion(bf16[2048,896]{1,0:T(8,128)(2,1)S(1)} %copy-done.6, bf16[768,4096]{1,0:T(8,128)(2,1)S(1)} %bitcast.26, bf16[768,2688]{1,0:T(8,128)(2,1)S(1)} %copy-done.12), kind=kOutput, calls=%fused_computation.2 | convolution fusion | flops 2824077312 | bytes 11862016 | tf_op jit(solution)/shard_map/dot_general | solution.py:20
  238.0 0.0 copy-done.7
  238.0 5.1 %multiply_convert_fusion.2 = bf16[2048,896]{1,0:T(8,128)(2,1)} fusion(bf16[2048,896]{1,0:T(8,128)(2,1)S(1)} %copy-done.7, bf16[768,4096]{1,0:T(8,128)(2,1)S(1)} %bitcast.26, bf16[768,2688]{1,0:T(8,128)(2,1)S(1)} %copy-done.12), kind=kOutput, calls=%fused_computation.3 | convolution fusion | flops 2824077312 | bytes 11862016 | tf_op jit(solution)/shard_map/dot_general | solution.py:20
  243.1 33.9 %all-to-all-done.1 = bf16[32,24,4096]{2,1,0:T(8,128)(2,1)} async-done(((bf16[32,24,4096]{2,1,0:T(8,128)(2,1)}), bf16[32,24,4096]{2,1,0:T(8,128)(2,1)}, u32[]{:S(2)}, u32[]{:S(2)}) %all-to-all-start.1) | async-done | bytes 6291488 | tf_op jit(solution)/shard_map/all_to_all | solution.py:75
  277.0 4.1 %reduce_sum.22 = bf16[24,4096]{1,0:T(8,128)(2,1)S(1)} reduce(bf16[32,24,4096]{2,1,0:T(8,128)(2,1)} %all-to-all-done.1, bf16[]{:T(256)} %constant.7.clone.1), dimensions={0}, to_apply=%region_1.2 | reduce | flops 3047424 | bytes 6488066 | tf_op jit(solution)/shard_map/reduce_sum | solution.py:80
  281.1 0.7 fusion.25
  (15 shorter events, 0.0 us)
Async XLA Ops:
  7.2 54.7 %all-gather.3.cloned.1.call-start = ((), (), s32[]{:S(2)}) async-start(), calls=%async_computation.2 | async-start | bytes 6488064 | tf_op jit(solution)/shard_map/all_gather | solution.py:40
  8.9 166.2 %all-gather.5.cloned.1.call-start = ((), (), s32[]{:S(2)}) async-start(), calls=%async_computation.3 | async-start | bytes 5160960 | tf_op jit(solution)/shard_map/all_gather | solution.py:62
  10.0 6.1 %copy-start.8 = (s32[32,14]{0,1:T(8,128)S(1)}, s32[32,14]{0,1:T(8,128)}, u32[]{:S(2)}) copy-start(s32[32,14]{0,1:T(8,128)} %param.13) | copy-start | bytes 5380
  16.4 6.1 %copy-start.9 = (s32[32,14]{0,1:T(8,128)S(1)}, s32[32,14]{0,1:T(8,128)}, u32[]{:S(2)}) copy-start(s32[32,14]{0,1:T(8,128)} %param.12) | copy-start | bytes 5380
  28.8 4.4 %copy-start = (bf16[2048,896]{0,1:T(8,128)(2,1)S(1)}, bf16[2048,896]{0,1:T(8,128)(2,1)}, u32[]{:S(2)}) copy-start(bf16[2048,896]{0,1:T(8,128)(2,1)} %copy.23) | copy-start | bytes 11010052
  33.2 3.4 %copy-start.1 = (bf16[2048,896]{0,1:T(8,128)(2,1)S(1)}, bf16[2048,896]{0,1:T(8,128)(2,1)}, u32[]{:S(2)}) copy-start(bf16[2048,896]{0,1:T(8,128)(2,1)} %copy.22) | copy-start | bytes 11010052
  61.9 6.5 %copy-start.2 = (bf16[2048,896]{0,1:T(8,128)(2,1)S(1)}, bf16[2048,896]{0,1:T(8,128)(2,1)}, u32[]{:S(2)}) copy-start(bf16[2048,896]{0,1:T(8,128)(2,1)} %bitcast_multiply_fusion.1) | copy-start | bytes 11010052
  61.9 6.6 %copy-start.10 = (bf16[768,4096]{1,0:T(8,128)(2,1)S(1)}, bf16[768,4096]{1,0:T(8,128)(2,1)}, u32[]{:S(2)}) copy-start(bf16[768,4096]{1,0:T(8,128)(2,1)} %all-gather.3.cloned.1.call-done) | copy-start | bytes 18874372
  68.4 3.5 %copy-start.4 = (bf16[2048,896]{0,1:T(8,128)(2,1)S(1)}, bf16[2048,896]{0,1:T(8,128)(2,1)}, u32[]{:S(2)}) copy-start(bf16[2048,896]{0,1:T(8,128)(2,1)} %bitcast_multiply_fusion.2) | copy-start | bytes 11010052
  175.1 6.1 %copy-start.5 = (bf16[2048,896]{0,1:T(8,128)(2,1)S(1)}, bf16[2048,896]{0,1:T(8,128)(2,1)}, u32[]{:S(2)}) copy-start(bf16[2048,896]{0,1:T(8,128)(2,1)} %bitcast_multiply_fusion.2) | copy-start | bytes 11010052
  175.1 6.1 %copy-start.11 = (bf16[768,2688]{1,0:T(8,128)(2,1)S(1)}, bf16[768,2688]{1,0:T(8,128)(2,1)}, u32[]{:S(2)}) copy-start(bf16[768,2688]{1,0:T(8,128)(2,1)} %all-gather.5.cloned.1.call-done) | copy-start | bytes 12386308
  181.2 3.4 %copy-start.3 = (bf16[2048,896]{0,1:T(8,128)(2,1)S(1)}, bf16[2048,896]{0,1:T(8,128)(2,1)}, u32[]{:S(2)}) copy-start(bf16[2048,896]{0,1:T(8,128)(2,1)} %bitcast_multiply_fusion.1) | copy-start | bytes 11010052
  191.8 85.2 %all-to-all-start.1 = ((bf16[32,24,4096]{2,1,0:T(8,128)(2,1)}), bf16[32,24,4096]{2,1,0:T(8,128)(2,1)}, u32[]{:S(2)}, u32[]{:S(2)}) async-start(bf16[32,24,4096]{2,1,0:T(8,128)(2,1)} %bitcast.20), calls=%async_computation.1 | async-start | bytes 12582912 | tf_op jit(solution)/shard_map/all_to_all | solution.py:75
  218.2 14.7 %slice-start = ((s8[6291456]{0:T(1024)(128)(4,1)}), s8[2097152]{0:T(1024)(128)(4,1)S(1)}, s32[]{:S(2)}) async-start(s8[6291456]{0:T(1024)(128)(4,1)} %bitcast.25), calls=%async_computation.4 | async-start | bytes 4194304
  224.4 8.5 %copy-start.6 = (bf16[2048,896]{1,0:T(8,128)(2,1)S(1)}, bf16[2048,896]{1,0:T(8,128)(2,1)}, u32[]{:S(2)}) copy-start(bf16[2048,896]{1,0:T(8,128)(2,1)} %copy.27) | copy-start | bytes 11010052
  224.4 8.5 %slice-start.1 = ((s8[6291456]{0:T(1024)(128)(4,1)}), s8[4194304]{0:T(1024)(128)(4,1)S(1)}, s32[]{:S(2)}) async-start(s8[6291456]{0:T(1024)(128)(4,1)} %bitcast.25), calls=%async_computation.5 | async-start | bytes 8388608
  224.4 8.5 %copy-start.12 = (bf16[768,2688]{1,0:T(8,128)(2,1)S(1)}, bf16[768,2688]{1,0:T(8,128)(2,1)}, u32[]{:S(2)}) copy-start(bf16[768,2688]{1,0:T(8,128)(2,1)} %all-gather.5.cloned.1.call-done) | copy-start | bytes 12386308
  232.9 5.1 %copy-start.7 = (bf16[2048,896]{1,0:T(8,128)(2,1)S(1)}, bf16[2048,896]{1,0:T(8,128)(2,1)}, u32[]{:S(2)}) copy-start(bf16[2048,896]{1,0:T(8,128)(2,1)} %copy.26) | copy-start | bytes 11010052
Sparse Core Ops, SparseCore 0:
  10.2 51.5 all-gather.2
  130.5 44.5 all-gather.4
